TPU v7x, 256 devices: a whole 4x4x8 slice. The times are simulated.
256 devices in a mesh: grp: 8 (over x, y_hi), row: 32 (over y_lo, z, core).
Axes of the slice: x: 4, y: 4 (y_hi: 2, y_lo: 2; y = y_hi * 2 + y_lo), z: 8, core: 2. Of those that a mesh axis runs over, the one named last changes fastest.
Arguments:
- blocks: bfloat16 [256, 8, 10, 256, 256], P(('grp', 'row')), may hold values from 0 to 1
- columns: int32 [256, 8, 10], P(('grp', 'row')), may hold values from -1 to 255, as said below
- factor: bfloat16 [64, 65536], P(None, ('grp', 'row')), may hold values from 0 to 0.3, as said below
Outputs:
- updated: float32 [64, 65536], P(None, ('grp', 'row'))
Inputs may be any that keep to these rules, and one draw needn't show every extreme that they name: Tile row i lies in group g = i // 32. In block h of tile row i the live slots come first and name distinct tile columns of group h (h * 32 to h * 32 + 31), none above i; block g always names i itself; blocks h > g are empty; a block holds at most 10 live slots, and -1 marks an empty slot. `factor`: entries are nonnegative.
All inputs are finite; a program needn't handle non-finite values.
Results may differ from a plain program's by a relative error of at most 0.0003.
Values may be sent and summed in bfloat16 or wider, within the bound.
A program may use at most 128 MiB of HBM per device.

v0:
```python
import jax
import jax.numpy as jnp
from jax import lax
from jax.sharding import Mesh
from jax.sharding import PartitionSpec as P

ROW = ("row_0", "row_1", "row_2")
GRP = ("grp_0", "grp_1")
GRP_ROW = ("grp_0", "grp_1", "row_0", "row_1", "row_2")


floor_value = 1e-06


def over_axes(value, axes):
    for axis in axes:
        value = lax.psum(value, axis)
    return value


def sent_to_all(value, axis):
    copies = jnp.broadcast_to(value, (lax.axis_size(axis), *value.shape))
    return lax.all_to_all(copies, axis, split_axis=0, concat_axis=0, tiled=True)


def in_order(tiles, dim):
    dims = list(tiles.shape[1:])
    dims[dim] *= tiles.shape[0]
    return jnp.moveaxis(tiles, 0, dim).reshape(dims)


def collect(value, axis, dim):
    tiles = sent_to_all(value, axis)
    return in_order(tiles, dim)


def in_blocks(value, dim, peers):
    dims = value.shape
    tiles = value.reshape(*dims[:dim], peers, dims[dim] // peers, *dims[dim + 1 :])
    return jnp.moveaxis(tiles, dim, 0)


def sent_and_summed(value, axis, dim):
    tiles = in_blocks(value, dim, lax.axis_size(axis))
    arrived = lax.all_to_all(tiles, axis, split_axis=0, concat_axis=0, tiled=True)
    return arrived.sum(axis=0)


def sweep(current, products, gram):

    def update(column, current):
        weights = lax.dynamic_index_in_dim(gram, column, 1, keepdims=False)
        fitted = jnp.dot(weights, current, precision=lax.Precision.HIGHEST)
        target = lax.dynamic_index_in_dim(products, column, 0, keepdims=False)
        present = lax.dynamic_index_in_dim(current, column, 0, keepdims=False)
        diagonal = gram[column, column]
        fresh = jnp.maximum(present + (target - fitted) / diagonal, floor_value)
        return lax.dynamic_update_index_in_dim(current, fresh, column, 0)

    return lax.fori_loop(0, current.shape[0], update, current)


def choose_rows(group_cols, group_number, rows_grp):
    offsets = group_cols - group_number * rows_grp
    positions = lax.broadcasted_iota(jnp.int32, (group_cols.shape[0], rows_grp), 1)
    return (offsets[:, None] == positions) & (group_cols >= 0)[:, None]


def lower_work(group_tiles, group_cols, group_number, group_factor, rows_grp):
    rank_count, span = group_factor.shape
    tile_size = span // rows_grp
    stacked = group_factor.reshape(rank_count, rows_grp, tile_size)
    selected = choose_rows(group_cols, group_number, rows_grp)
    fetched = jnp.einsum(
        "sn,rnt->srt", selected.astype(jnp.bfloat16), stacked, preferred_element_type=jnp.float32
    ).astype(jnp.bfloat16)
    return jnp.einsum("srv,suv->ru", fetched, group_tiles, preferred_element_type=jnp.float32)


def per_device(blocks, columns, factor):
    tiles_dev = blocks[0]
    cols_dev = columns[0]
    rank_count, tile_size = factor.shape
    rows_grp = lax.axis_size(ROW)
    group_count = lax.axis_size(GRP)
    span = rows_grp * tile_size
    gram = over_axes(jnp.dot(factor, factor.T, preferred_element_type=jnp.float32), GRP_ROW)
    group_factor = collect(factor, ROW, 1)
    my_group = lax.axis_index(GRP)
    slot_count = cols_dev.shape[1]
    live = (cols_dev >= 0).astype(jnp.float32)
    mirror = jnp.einsum("ru,hsuv->hsrv", factor, tiles_dev, preferred_element_type=jnp.float32)
    mirror = mirror * live[:, :, None, None]
    arrived, arrived_cols = (
        lax.all_to_all(mirror, GRP, split_axis=0, concat_axis=0, tiled=True),
        lax.all_to_all(cols_dev, GRP, split_axis=0, concat_axis=0, tiled=True),
    )
    flat_cols = arrived_cols.reshape(group_count * slot_count)
    selected = choose_rows(flat_cols, my_group, rows_grp).astype(jnp.float32)
    flat_mirror = arrived.reshape(group_count * slot_count, rank_count, tile_size)
    spread = jnp.einsum("sn,srv->rnv", selected, flat_mirror, precision=lax.Precision.HIGHEST)
    mirror_sum = sent_and_summed(spread.reshape(rank_count, span), ROW, 1)
    lower_sum = jnp.zeros((rank_count, tile_size), jnp.float32)
    piece = lax.all_gather(group_factor, GRP, axis=1, tiled=True)
    begin_at = jnp.int32(0)
    for offset in range(piece.shape[1] // span):
        group_number = begin_at // span + offset
        group_tiles = lax.dynamic_index_in_dim(tiles_dev, group_number, 0, keepdims=False)
        group_cols = lax.dynamic_index_in_dim(cols_dev, group_number, 0, keepdims=False)
        block_cols = lax.dynamic_slice_in_dim(piece, offset * span, span, 1)
        lower_sum = lower_sum + lower_work(
            group_tiles, group_cols, group_number, block_cols, rows_grp
        )
    products = lower_sum + mirror_sum
    return sweep(factor.astype(jnp.float32), products, gram)


def solution(mesh):
    split = Mesh(mesh.devices.reshape(4, 2, 2, 8, 2), ("grp_0", "grp_1", "row_0", "row_1", "row_2"))
    placed = (P(GRP_ROW, None, None, None, None), P(GRP_ROW, None, None), P(None, GRP_ROW))
    return jax.shard_map(
        per_device, mesh=split, in_specs=placed, out_specs=P(None, GRP_ROW), check_vma=False
    )
```

profile of v0, /device:TPU:32, one launch (start us, length us, event | category | flops | bytes accessed | tf_op | source)
XLA Modules:
  0.0 372.1 jit_solution(12893617973053168227)
XLA Ops:
  6.5 0.9 broadcast_in_dim.9
  7.5 38.5 %all_to_all.24 = bf16[32,64,256]{2,1,0:T(8,128)(2,1)S(1)} all-to-all(bf16[32,64,256]{2,1,0:T(8,128)(2,1)S(1)} %broadcast_in_dim.9), channel_id=1, replica_groups=mesh['grp_0'=4,'grp_1'=2,'row_0'=2,'row_1'=8,'row_2'=2] {'row_0','row_1'..., dimensions={0} | all-to-all | bytes 2097152 | tf_op jit(solution)/shard_map/all_to_all | solution.py:23
  46.0 1.1 copy.35
  47.1 6.6 %all-to-all-start.1 = ((s32[8,1,10]{2,1,0:T(1,128)}), s32[8,1,10]{2,1,0:T(1,128)S(1)}, u32[]{:S(2)}, u32[]{:S(2)}) async-start(s32[8,1,10]{2,1,0:T(1,128)} %bitcast.47), calls=%async_computation.1 | async-start | bytes 8192 | tf_op jit(solution)/shard_map/all_to_all | solution.py:96
  53.7 0.7 convert_bitcast_fusion
  54.4 9.0 %multiply_bitcast_fusion = f32[8,10,64,256]{3,2,1,0:T(8,128)} fusion(f32[8,10]{1,0:T(8,128)S(1)} %convert_bitcast_fusion, bf16[1,8,10,256,256]{4,3,2,1,0:T(8,128)(2,1)} %param.5, bf16[64,256]{1,0:T(8,128)(2,1)S(1)} %copy-done.1), kind=kOutput, calls=%fused_computation.10 | convolution fusion | flops 672399360 | bytes 15761728 | tf_op jit(solution)/shard_map/ru,hsuv->hsrv/dot_general | solution.py:92
  63.4 7.5 %all-to-all-start.2 = ((f32[8,10,64,256]{3,2,1,0:T(8,128)}), f32[8,10,64,256]{3,2,1,0:T(8,128)}, u32[]{:S(2)}, u32[]{:S(2)}) async-start(f32[8,10,64,256]{3,2,1,0:T(8,128)} %multiply_bitcast_fusion), calls=%async_computation.2 | async-start | bytes 10485760 | tf_op jit(solution)/shard_map/all_to_all | solution.py:95
  71.1 77.4 %all-to-all-done.2 = f32[8,10,64,256]{3,2,1,0:T(8,128)} async-done(((f32[8,10,64,256]{3,2,1,0:T(8,128)}), f32[8,10,64,256]{3,2,1,0:T(8,128)}, u32[]{:S(2)}, u32[]{:S(2)}) %all-to-all-start.2) | async-done | bytes 5242912 | tf_op jit(solution)/shard_map/all_to_all | solution.py:95
  148.6 7.2 %fusion.4 = f32[32,64,256]{2,0,1:T(8,128)S(1)} fusion(f32[80,64,256]{2,1,0:T(8,128)} %bitcast.54, s32[80]{0:T(128)S(1)} %sub.103, pred[80]{0:T(512)(128)(4,1)S(1)} %ge.118), kind=kOutput, calls=%fused_computation.8 | convolution fusion | flops 503321600 | bytes 7340432 | tf_op jit(solution)/shard_map/sn,srv->rnv/dot_general | solution.py:101
  155.8 2.6 copy.32
  158.4 13.4 %all-to-all-start.3 = ((f32[32,64,256]{2,1,0:T(8,128)}), f32[32,64,256]{2,1,0:T(8,128)S(1)}, u32[]{:S(2)}, u32[]{:S(2)}) async-start(f32[32,64,256]{2,1,0:T(8,128)} %copy.32), calls=%async_computation.3 | async-start | bytes 4194304 | tf_op jit(solution)/shard_map/all_to_all | solution.py:45
  172.0 16.4 %psum.35 = f32[64,64]{1,0:T(8,128)S(1)} all-reduce(f32[64,64]{1,0:T(8,128)S(1)} %fusion.135), channel_id=1, replica_groups=mesh['grp_0'=4,'grp_1'=2,'row_0'=2,'row_1'=8,'row_2'=2] {'grp_0'}, use_global_device_ids=true, to_apply=%region_0.0 | all-reduce | flops 4096 | bytes 32768 | tf_op jit(solution)/shard_map/psum | solution.py:17
  188.3 11.9 %psum.36 = f32[64,64]{1,0:T(8,128)S(1)} all-reduce(f32[64,64]{1,0:T(8,128)S(1)} %psum.35), channel_id=1, replica_groups=mesh['grp_0'=4,'grp_1'=2,'row_0'=2,'row_1'=8,'row_2'=2] {'grp_1'}, use_global_device_ids=true, to_apply=%region_1.0 | all-reduce | flops 4096 | bytes 32768 | tf_op jit(solution)/shard_map/psum | solution.py:17
  200.3 12.6 %psum.37 = f32[64,64]{1,0:T(8,128)S(1)} all-reduce(f32[64,64]{1,0:T(8,128)S(1)} %psum.36), channel_id=1, replica_groups=mesh['grp_0'=4,'grp_1'=2,'row_0'=2,'row_1'=8,'row_2'=2] {'row_0'}, use_global_device_ids=true, to_apply=%region_2.0 | all-reduce | flops 4096 | bytes 32768 | tf_op jit(solution)/shard_map/psum | solution.py:17
  212.9 28.0 %psum.38 = f32[64,64]{1,0:T(8,128)S(1)} all-reduce(f32[64,64]{1,0:T(8,128)S(1)} %psum.37), channel_id=1, replica_groups=mesh['grp_0'=4,'grp_1'=2,'row_0'=2,'row_1'=8,'row_2'=2] {'row_1'}, use_global_device_ids=true, to_apply=%region_3.0 | all-reduce | flops 4096 | bytes 32768 | tf_op jit(solution)/shard_map/psum | solution.py:17
  240.8 3.6 psum.39
  244.5 0.7 broadcast_compare_fusion
  245.2 1.0 compare_bitcast_fusion
  246.2 1.0 add_bitcast_fusion
  247.3 3.9 %fusion.134 = (bf16[64,8192]{1,0:T(8,128)(2,1)S(1)}, bf16[64,8192]{1,0:T(8,128)(2,1)S(1)}, bf16[64,8192]{1,0:T(8,128)(2,1)S(1)}, bf16[64,8192]{1,0:T(8,128)(2,1)...) fusion(bf16[64,65536]{1,0:T(8,128)(2,1)} %all-gather.2.cloned.1, ...), kind=kLoop, calls=%fused_computation.132 | loop fusion | bytes 16777216 | tf_op jit(solution)/shard_map/dynamic_slice | solution.py:110
  252.1 2.2 fusion.32
  262.4 102.2 %while.13 = (s32[]{:T(128)}, f32[64,256]{1,0:T(8,128)S(1)}, f32[64,256]{1,0:T(8,128)S(1)}, f32[64,64]{0,1:T(8,128)S(1)}, s32[]{:T(128)}, /*index=5*/s32[]{:T(128)}) while((s32[]{:T(128)}, f32[64,256]{1,0:T(8,128)S(1)}, f32[64,256]{1,0:T(8,128)S(1)}, f32[64,64]{0,1:T(8,128)S(1)}, s32[]{:T(128)}, /*index=5*/s32[]{:T(128)}) %tuple.55), condition=%wide.region_7.8_spmd, body=%wide.region_6.7_spmd.sunk | while | flops 197634 | bytes 77409 | solution.py:60
  264.9 0.7 fusion.152
  268.1 0.7 fusion.152
  272.8 0.7 fusion.152
  276.0 0.7 fusion.152
  279.2 0.7 fusion.152
  280.8 0.7 fusion.152
  284.0 0.7 fusion.152
  287.2 0.7 fusion.152
  290.4 0.7 fusion.152
  292.0 0.7 fusion.152
  (357 shorter events, 103.1 us)
Async XLA Ops:
  6.5 47.9 %copy-start.1 = (bf16[64,256]{1,0:T(8,128)(2,1)S(1)}, bf16[64,256]{1,0:T(8,128)(2,1)}, u32[]{:S(2)}) copy-start(bf16[64,256]{1,0:T(8,128)(2,1)} %param.7) | copy-start | bytes 98308
  6.5 240.8 %all-gather.2.cloned.1.call-start = ((), (), s32[]{:S(2)}) async-start(), calls=%async_computation.4 | async-start | bytes 9437184 | tf_op jit(solution)/shard_map/all_gather | solution.py:104
  47.1 16.4 %all-to-all-start.1 = ((s32[8,1,10]{2,1,0:T(1,128)}), s32[8,1,10]{2,1,0:T(1,128)S(1)}, u32[]{:S(2)}, u32[]{:S(2)}) async-start(s32[8,1,10]{2,1,0:T(1,128)} %bitcast.47), calls=%async_computation.1 | async-start | bytes 8192 | tf_op jit(solution)/shard_map/all_to_all | solution.py:96
  63.4 85.1 %all-to-all-start.2 = ((f32[8,10,64,256]{3,2,1,0:T(8,128)}), f32[8,10,64,256]{3,2,1,0:T(8,128)}, u32[]{:S(2)}, u32[]{:S(2)}) async-start(f32[8,10,64,256]{3,2,1,0:T(8,128)} %multiply_bitcast_fusion), calls=%async_computation.2 | async-start | bytes 10485760 | tf_op jit(solution)/shard_map/all_to_all | solution.py:95
  158.4 88.8 %all-to-all-start.3 = ((f32[32,64,256]{2,1,0:T(8,128)}), f32[32,64,256]{2,1,0:T(8,128)S(1)}, u32[]{:S(2)}, u32[]{:S(2)}) async-start(f32[32,64,256]{2,1,0:T(8,128)} %copy.32), calls=%async_computation.3 | async-start | bytes 4194304 | tf_op jit(solution)/shard_map/all_to_all | solution.py:45
  251.2 5.0 %slice-start = ((s8[10485760]{0:T(1024)(128)(4,1)}), s8[4194304]{0:T(1024)(128)(4,1)S(1)}, s32[]{:S(2)}) async-start(s8[10485760]{0:T(1024)(128)(4,1)} %bitcast.213), calls=%async_computation.5 | async-start | bytes 8388608
  252.1 4.2 %slice-start.1 = ((s8[10485760]{0:T(1024)(128)(4,1)}), s8[4194304]{0:T(1024)(128)(4,1)S(1)}, s32[]{:S(2)}) async-start(s8[10485760]{0:T(1024)(128)(4,1)} %bitcast.213), calls=%async_computation.6 | async-start | bytes 8388608
  255.1 1.6 slice-start.2
  364.7 0.6 copy-start
Sparse Core Ops, SparseCore 0:
  47.2 164.4 all-gather.1
where the time goes:
time: 377 us; the launch traced here: 372 us
  blocking collectives  111 us (29%)
  waiting for transfers between devices  77.5 us (21%)
  local copies, waits for them, and re-layouts  58.2 us (15%)
  other arithmetic  48 us (13%)
  matrix products  34 us (9%)
  starting transfers between devices  27.6 us (7%)
  between operations  13.7 us (4%)
    all_to_all x1, waiting for transfers between devices, per_device(): lax.all_to_all(mirror, GRP, split_axis=0, concat_axis=0, tiled=True)  77.4 us
    psum x5, blocking collectives, over_axes(): value = lax.psum(value, axis)  72.4 us
    max x64, other arithmetic, update(): fresh = jnp.maximum(present + (target - fitted) / diagonal, floor_value)  44.4 us
    dynamic_slice x64, local copies, waits for them, and re-layouts, update(): diagonal = gram[column, column]  42.9 us
    all_to_all x1, blocking collectives, sent_to_all(): return lax.all_to_all(copies, axis, split_axis=0, concat_axis=0, tiled=True)  38.5 us
    all_to_all x1, starting transfers between devices, sent_and_summed(): lax.all_to_all(tiles, axis, split_axis=0, concat_axis=0, tiled=True)  13.4 us
    dot_general x64, matrix products, update(): fitted = jnp.dot(weights, current, precision=lax.Precision.HIGHEST)  9.16 us
    dot_general x1, matrix products, per_device(): jnp.einsum('ru,hsuv->hsrv', factor, tiles_dev, preferred_element_type=jnp...  8.99 us
  transfers between devices with their start and end apart: 4, of which 1 were waited for; matrix products, arithmetic and copies ran while one was open for 6% of the time, Pallas kernels for 0%

commit v1 on v0

v1 whole, which is shorter than its diff:
```python
import functools

import jax
import jax.numpy as jnp
from jax import lax
from jax.experimental import pallas as pl
from jax.experimental.pallas import tpu as pltpu
from jax.sharding import Mesh
from jax.sharding import PartitionSpec as P

AXES = ("grp_0", "grp_1", "row_0", "row_1", "row_2")
BY_MESH = pl.DeviceIdType.MESH
LANES = 128
INV_LANE = 32
LEVELS = 65534.0
OFFSET = 32768.0
floor_value = 1e-6


def nt_dot(a, b):
    return lax.dot_general(a, b, (((1,), (1,)), ((), ())), preferred_element_type=jnp.float32)


def to_column(row, rank):
    spread = jnp.broadcast_to(row, (rank, LANES))
    lane = lax.broadcasted_iota(jnp.int32, (rank, LANES), 1)
    place = lax.broadcasted_iota(jnp.int32, (rank, LANES), 0)
    return jnp.sum(jnp.where(lane == place, spread, 0.0), axis=1, keepdims=True)


def exchange_kernel(
    sizes,
    blocks,
    cols,
    factor,
    prod_out,
    gram_out,
    tiles,
    hall,
    tab,
    tabin,
    tabs,
    sums,
    sumsin,
    scale,
    base,
    sendm,
    recvm,
    ownm,
    sendl,
    recvl,
    lower,
    gsend,
    grecv,
    part,
    cbuf,
    crecv,
    yrecv,
    zrecv,
    blk_sem,
    tab_sem,
    ag_s,
    ag_r,
    tab_s,
    tab_r,
    sum_s,
    sum_r,
    m_s,
    m_r,
    l_s,
    l_r,
    g_s,
    g_r,
    c_s,
    c_r,
    y_s,
    y_r,
    z_s,
    z_r,
):
    _, ngy, nry, nrz, nrc = sizes
    gx, gy, ry, rz, rc = [lax.axis_index(axis) for axis in AXES]
    groups, slots = tiles.shape[0], tiles.shape[1]
    rank, tile = factor.shape
    rows_grp = nry * nrz * nrc
    me = gx * ngy + gy

    def place(y, z, c):
        return (y * nrz + z) * nrc + c

    mine = place(ry, rz, rc)

    def group_peer(h):
        hx, hy = h // ngy, h % ngy
        flip = (hy - gy) * (hy - gy)
        return (hx, hy, ry + flip - 2 * ry * flip, rz, rc)

    def z_peer(z):
        return (gx, gy, ry, z, rc)

    y_peer = (gx, gy, 1 - ry, rz, rc)
    c_peer = (gx, gy, ry, rz, 1 - rc)

    def z_other(i):
        step = (i // 2 + 1) * (1 - 2 * (i % 2))
        return (rz + step + nrz) % nrz

    def remote(src, dst, send, recv, peer):
        return pltpu.make_async_remote_copy(
            src_ref=src, dst_ref=dst, send_sem=send, recv_sem=recv, device_id=peer, device_id_type=BY_MESH
        )

    def block_copy(h):
        return pltpu.make_async_copy(blocks.at[0, h], tiles.at[h], blk_sem.at[h])

    def loop(start, stop, body):
        def step(i, carry):
            body(i)
            return carry

        lax.fori_loop(start, stop, step, 0)

    loop(0, me + 1, lambda h: block_copy(h).start())

    hall[mine] = factor[...]
    hall[rows_grp] = jnp.zeros((rank, tile), hall.dtype)
    ownm[slots] = jnp.zeros((rank, tile), jnp.float32)
    for g in range(groups):
        recvm[g, slots] = jnp.full((rank, tile), -OFFSET, jnp.float32).astype(jnp.int32).astype(recvm.dtype)
    all_cols = cols[0]
    lane = lax.broadcasted_iota(jnp.int32, (groups, LANES), 1)
    row = lax.broadcasted_iota(jnp.int32, (groups, LANES), 0)
    table = jnp.where(lane >= INV_LANE, slots, rows_grp)
    for s in range(slots):
        column = jnp.broadcast_to(all_cols[:, s : s + 1], (groups, LANES))
        offset = column - row * rows_grp
        live = (offset >= 0) & (offset < rows_grp)
        table = jnp.where(live & (lane == s), offset, table)
        table = jnp.where(live & (lane - INV_LANE == offset), s, table)
    for h in range(groups):
        tab[h] = jnp.broadcast_to(table[h : h + 1], (8, LANES))
        tabin[h] = jnp.zeros((8, LANES), jnp.int32)
    tabin[me] = tab[me]
    row_sums = nt_dot(jnp.ones((8, tile), jnp.bfloat16), factor[...])
    sums[...] = jnp.zeros((8, LANES), jnp.float32)
    sums[:, 0:rank] = jnp.maximum(row_sums, 1e-30)
    to_levels = LEVELS / to_column(sums[0:1, :], rank)

    barrier = pltpu.get_barrier_semaphore()

    def greet(peer):
        pl.semaphore_signal(barrier, inc=1, device_id=peer, device_id_type=BY_MESH)

    loop(0, me, lambda h: greet(group_peer(h)))
    loop(me + 1, groups, lambda h: greet(group_peer(h)))
    loop(0, nrz - 1, lambda i: greet(z_peer(z_other(i))))
    greet(y_peer)
    greet(c_peer)
    pl.semaphore_wait(barrier, groups - 1 + nrz - 1 + 2)

    def z_send(z):
        return remote(factor, hall.at[mine], ag_s.at[z], ag_r.at[mine], z_peer(z))

    def y_send(z, src):
        p = place(ry, z, rc)
        return remote(src, hall.at[p], ag_s.at[nrz + z], ag_r.at[p], y_peer)

    def c_send(y, z, src):
        p = place(y, z, rc)
        return remote(src, hall.at[p], ag_s.at[2 * nrz + y * nrz + z], ag_r.at[p], c_peer)

    def arrived(p):
        remote(factor, hall.at[p], ag_s.at[0], ag_r.at[p], c_peer).wait_recv()

    loop(0, nrz - 1, lambda i: z_send(z_other(i)).start())
    y_send(rz, factor).start()
    c_send(ry, rz, factor).start()

    def table_send(h):
        return remote(tab.at[h], tabin.at[me], tab_s.at[h], tab_r.at[me], group_peer(h))

    def sums_send(h):
        return remote(sums, sumsin.at[me], sum_s.at[h], sum_r.at[me], group_peer(h))

    def small_sends(h):
        table_send(h).start()
        sums_send(h).start()

    loop(0, me, small_sends)

    def mirror_send(h):
        return remote(
            sendm.at[h], recvm.at[me, pl.ds(0, slots)], m_s.at[h], m_r.at[me], group_peer(h)
        )

    def mirror(h):
        block_copy(h).wait()
        for s in range(slots):
            product = jnp.dot(factor[...], tiles[h, s], preferred_element_type=jnp.float32)
            coded = jnp.round(product * to_levels - OFFSET)
            sendm[h, s] = coded.astype(jnp.int32).astype(sendm.dtype)
        mirror_send(h).start()

    def forward(i):
        z = z_other(i)
        p = place(ry, z, rc)
        arrived(p)
        y_send(z, hall.at[p]).start()
        c_send(ry, z, hall.at[p]).start()

    def first_step(i):
        @pl.when(i < me)
        def _():
            mirror(i)

        @pl.when(i < nrz - 1)
        def _():
            forward(i)

    loop(0, max(groups - 1, nrz - 1), first_step)

    def second_step(i):
        z = (rz + i) % nrz
        p = place(1 - ry, z, rc)
        arrived(p)
        c_send(1 - ry, z, hall.at[p]).start()

    loop(0, nrz, second_step)

    def tables_in(g):
        remote(tab.at[0], tabin.at[g], tab_s.at[0], tab_r.at[g], c_peer).wait_recv()
        remote(sums, sumsin.at[g], sum_s.at[0], sum_r.at[g], c_peer).wait_recv()
        column = to_column(sumsin[g][0:1, :], rank) * (1.0 / LEVELS)
        scale[g] = jnp.broadcast_to(column, (rank, tile))

    loop(me + 1, groups, tables_in)
    to_scalars = pltpu.make_async_copy(tabin, tabs, tab_sem)
    to_scalars.start()
    to_scalars.wait()
    loop(0, nry * nrz, lambda j: arrived(j * nrc + 1 - rc))

    def lower_send(g):
        return remote(sendl.at[g], recvl.at[me], l_s.at[g], l_r.at[me], group_peer(g))

    def serve(g):
        for s in range(slots):
            sendl[g, s] = hall[tabs[g, 0, s]]
        lower_send(g).start()

    loop(me + 1, groups, serve)

    def gram_step(p, total):
        return total + nt_dot(hall[p], hall[p])

    group_gram = lax.fori_loop(0, rows_grp, gram_step, jnp.zeros((rank, rank), jnp.float32))
    gsend[...] = jnp.zeros((rank, LANES), jnp.float32)
    gsend[:, 0:rank] = group_gram
    grecv[me] = gsend[...]

    block_copy(me).wait()
    lower[...] = jnp.zeros((rank, tile), jnp.float32)
    for s in range(slots):
        ownm[s] = jnp.dot(factor[...], tiles[me, s], preferred_element_type=jnp.float32)
        lower[...] += nt_dot(hall[tabs[me, 0, s]], tiles[me, s])

    def gram_send(h):
        return remote(gsend, grecv.at[me], g_s.at[h], g_r.at[me], group_peer(h))

    loop(0, me, lambda h: gram_send(h).start())
    loop(me + 1, groups, lambda h: gram_send(h).start())

    base[...] = jnp.zeros((rank, tile), jnp.float32)

    def mirror_in(g):
        remote(sendm.at[0], recvm.at[g, pl.ds(0, slots)], m_s.at[0], m_r.at[g], c_peer).wait_recv()
        base[...] += OFFSET * scale[g]

    loop(me + 1, groups, mirror_in)

    def summed(p):
        def add(g, total):
            coded = recvm[g, tabs[g, 0, INV_LANE + p]].astype(jnp.int32).astype(jnp.float32)
            return total + coded * scale[g]

        return lax.fori_loop(me + 1, groups, add, base[...] + ownm[tabs[me, 0, INV_LANE + p]])

    def core_send(j):
        return remote(cbuf.at[j], crecv.at[j], c_s.at[j], c_r.at[j], c_peer)

    def for_other(j):
        cbuf[j] = summed(j * nrc + 1 - rc)
        core_send(j).start()

    def for_this(j):
        part[j] = summed(j * nrc + rc)

    loop(0, nry * nrz, for_other)
    loop(0, nry * nrz, for_this)

    def row_y_send(z):
        return remote(part.at[(1 - ry) * nrz + z], yrecv.at[z], y_s.at[z], y_r.at[z], y_peer)

    def to_y(i):
        z = (rz + i) % nrz
        j = (1 - ry) * nrz + z
        core_send(j).wait_recv()
        part[j] += crecv[j]
        row_y_send(z).start()

    loop(0, nrz, to_y)

    def row_z_send(z):
        return remote(part.at[ry * nrz + z], zrecv.at[rz], z_s.at[z], z_r.at[rz], z_peer(z))

    def to_z(z):
        j = ry * nrz + z
        core_send(j).wait_recv()
        row_y_send(z).wait_recv()
        part[j] += crecv[j] + yrecv[z]

    def to_z_sent(i):
        z = z_other(i)
        to_z(z)
        row_z_send(z).start()

    loop(0, nrz - 1, to_z_sent)
    to_z(rz)

    def lower_in(h):
        remote(sendl.at[0], recvl.at[h], l_s.at[0], l_r.at[h], c_peer).wait_recv()
        total = lower[...]
        for s in range(slots):
            total += nt_dot(recvl[h, s], tiles[h, s])
        lower[...] = total

    loop(0, me, lower_in)

    lower[...] += part[ry * nrz + rz]

    def from_z(i):
        z = z_other(i)
        remote(part.at[0], zrecv.at[z], z_s.at[0], z_r.at[z], c_peer).wait_recv()
        lower[...] += zrecv[z]

    loop(0, nrz - 1, from_z)
    prod_out[...] = lower[...]

    def gram_in(g):
        remote(gsend, grecv.at[g], g_s.at[0], g_r.at[g], c_peer).wait_recv()

    loop(0, me, gram_in)
    loop(me + 1, groups, gram_in)
    total = grecv[0]
    for g in range(1, groups):
        total += grecv[g]
    gram_out[...] = total

    def sent_down(h):
        table_send(h).wait_send()
        sums_send(h).wait_send()
        mirror_send(h).wait_send()
        gram_send(h).wait_send()

    def sent_up(g):
        lower_send(g).wait_send()
        gram_send(g).wait_send()

    loop(0, me, sent_down)
    loop(me + 1, groups, sent_up)

    def sent_z(i):
        z = z_other(i)
        z_send(z).wait_send()
        row_z_send(z).wait_send()

    loop(0, nrz - 1, sent_z)

    def sent_y(z):
        y_send(z, factor).wait_send()
        row_y_send(z).wait_send()

    loop(0, nrz, sent_y)

    def sent_c(j):
        c_send(j // nrz, j % nrz, factor).wait_send()
        core_send(j).wait_send()

    loop(0, nry * nrz, sent_c)


def exchange(sizes, blocks, columns, factor):
    _, groups, slots, tile, _ = blocks.shape
    rank = factor.shape[0]
    _, _, nry, nrz, nrc = sizes
    rows_grp = nry * nrz * nrc
    pairs = nry * nrz
    f32, bf16, i32, i16 = jnp.float32, jnp.bfloat16, jnp.int32, jnp.int16
    dma = pltpu.SemaphoreType.DMA
    one = (rank, tile)
    vmem = pl.BlockSpec(memory_space=pltpu.VMEM)
    return pl.pallas_call(
        functools.partial(exchange_kernel, sizes),
        out_shape=(jax.ShapeDtypeStruct(one, f32), jax.ShapeDtypeStruct((rank, LANES), f32)),
        in_specs=[pl.BlockSpec(memory_space=pl.ANY), vmem, vmem],
        out_specs=(vmem, vmem),
        scratch_shapes=[
            pltpu.VMEM((groups, slots, tile, tile), bf16),
            pltpu.VMEM((rows_grp + 1, *one), bf16),
            pltpu.VMEM((groups, 8, LANES), i32),
            pltpu.VMEM((groups, 8, LANES), i32),
            pltpu.SMEM((groups, 8, LANES), i32),
            pltpu.VMEM((8, LANES), f32),
            pltpu.VMEM((groups, 8, LANES), f32),
            pltpu.VMEM((groups, *one), f32),
            pltpu.VMEM(one, f32),
            pltpu.VMEM((groups, slots, *one), i16),
            pltpu.VMEM((groups, slots + 1, *one), i16),
            pltpu.VMEM((slots + 1, *one), f32),
            pltpu.VMEM((groups, slots, *one), bf16),
            pltpu.VMEM((groups, slots, *one), bf16),
            pltpu.VMEM(one, f32),
            pltpu.VMEM((rank, LANES), f32),
            pltpu.VMEM((groups, rank, LANES), f32),
            pltpu.VMEM((pairs, *one), f32),
            pltpu.VMEM((pairs, *one), f32),
            pltpu.VMEM((pairs, *one), f32),
            pltpu.VMEM((nrz, *one), f32),
            pltpu.VMEM((nrz, *one), f32),
            dma((groups,)),
            dma,
            dma((2 * nrz + pairs,)),
            dma((rows_grp,)),
            *[dma((groups,))] * 10,
            *[dma((pairs,))] * 2,
            *[dma((nrz,))] * 4,
        ],
        compiler_params=pltpu.CompilerParams(
            collective_id=0, has_side_effects=True, vmem_limit_bytes=48 * 1024 * 1024
        ),
        name="exchange",
    )(blocks, columns, factor)


def sweep_kernel(products, gram, factor, out):
    rank, tile = factor.shape
    current = factor[...].astype(jnp.float32)
    gram_all = gram[:, 0:rank]
    fitted = lax.dot_general(
        gram_all,
        current,
        (((0,), (0,)), ((), ())),
        precision=lax.Precision.HIGHEST,
        preferred_element_type=jnp.float32,
    )
    excess = products[...] - fitted
    place = lax.broadcasted_iota(jnp.int32, (rank, rank), 0)
    lane = lax.broadcasted_iota(jnp.int32, (rank, rank), 1)
    diagonal = jnp.sum(jnp.where(place == lane, gram_all, 0.0), axis=1, keepdims=True)
    inverse = 1.0 / diagonal
    for k in range(rank):
        first = k // 8 * 8
        at = k - first
        present = current[k : k + 1]
        fresh = jnp.maximum(present + excess[at : at + 1] * inverse[k : k + 1], floor_value)
        out[k : k + 1, :] = fresh
        if k + 1 < rank:
            change = fresh - present
            keep = 8 if at == 7 else 0
            excess = excess[keep:] - gram_all[first + keep :, k : k + 1] * change


def sweep(products, gram, factor):
    return pl.pallas_call(
        sweep_kernel,
        out_shape=jax.ShapeDtypeStruct(factor.shape, jnp.float32),
        name="sweep",
    )(products, gram, factor)


def solution(mesh):
    groups, rows_grp = mesh.shape["grp"], mesh.shape["row"]
    sizes = (groups // 2, 2, 2, rows_grp // 4, 2)
    split = Mesh(mesh.devices.reshape(sizes), AXES)

    def per_device(blocks, columns, factor):
        products, gram = exchange(sizes, blocks, columns, factor)
        return sweep(products, gram, factor)

    placed = (P(AXES, None, None, None, None), P(AXES, None, None), P(None, AXES))
    return jax.shard_map(
        per_device, mesh=split, in_specs=placed, out_specs=P(None, AXES), check_vma=False
    )
```

time: 377 us -> 84.1 us (0.22)
  the two profiles are of different devices: /device:TPU:32 before, /device:TPU:60 now
where the time goes in v1:
time: 84.1 us; the launch traced here: 83.9 us
  Pallas kernels  81.2 us (97%)
  local copies, waits for them, and re-layouts  2.66 us (3%)
    pallas_call x1, Pallas kernels, exchange(): pl.pallas_call(functools.partial(exchange_kernel, sizes), out_shape=(jax....  79 us
    unnamed x8, local copies, waits for them, and re-layouts  2.66 us
    pallas_call x1, Pallas kernels, sweep(): pl.pallas_call(sweep_kernel, out_shape=jax.ShapeDtypeStruct(factor.shape,...  2.23 us

profile of v1, /device:TPU:60, one launch (start us, length us, event | category | flops | bytes accessed | tf_op | source)
XLA Modules:
  0.0 83.9 jit_solution(279222438221555110)
XLA Ops:
  0.0 0.0 copy-start
  0.0 0.8 copy-done
  0.8 0.0 copy-start.3
  0.8 0.7 copy-done.3
  1.4 79.0 %exchange.1 = (f32[64,256]{1,0:T(8,128)S(1)}, f32[64,128]{1,0:T(8,128)S(1)}) custom-call(bf16[1,8,10,256,256]{4,3,2,1,0:T(8,128)(2,1)} %blocks.1, s32[1,8,10]{2,1,0:T(8,128)S(1)} %copy-done.3, bf16[64,256]{1,0:T(8,128)(2,1)S(1)} %copy-done), custom_call_target="tpu_custom_call" | custom-call | tf_op jit(solution)/shard_map/exchange/pallas_call | solution.py:401
  80.5 0.0 copy-start.1
  80.5 0.6 copy-done.1
  81.1 0.0 copy-start.2
  81.1 0.6 copy-done.2
  81.7 2.2 %sweep.1 = f32[64,256]{1,0:T(8,128)} custom-call(f32[64,256]{1,0:T(8,128)} %copy-done.1, f32[64,128]{1,0:T(8,128)} %copy-done.2, bf16[64,256]{1,0:T(8,128)(2,1)} %factor.3), custom_call_target="tpu_custom_call" | custom-call | tf_op jit(solution)/shard_map/sweep/pallas_call | solution.py:473
Async XLA Ops:
  0.0 0.8 copy-start
  0.8 0.7 copy-start.3
  80.5 0.6 copy-start.1
  81.1 0.6 copy-start.2

commit v2 on v1

--- a/solution.py
+++ b/solution.py
@@ -12,6 +12,7 @@
 BY_MESH = pl.DeviceIdType.MESH
 LANES = 128
 INV_LANE = 32
+CHUNKS = 4
 LEVELS = 65534.0
 OFFSET = 32768.0
 floor_value = 1e-6
@@ -89,6 +90,8 @@
         return (y * nrz + z) * nrc + c
 
     mine = place(ry, rz, rc)
+    deep = rank // CHUNKS
+    half = nrz
 
     def group_peer(h):
         hx, hy = h // ngy, h % ngy
@@ -124,9 +127,11 @@
 
     hall[mine] = factor[...]
     hall[rows_grp] = jnp.zeros((rank, tile), hall.dtype)
-    ownm[slots] = jnp.zeros((rank, tile), jnp.float32)
     for g in range(groups):
-        recvm[g, slots] = jnp.full((rank, tile), -OFFSET, jnp.float32).astype(jnp.int32).astype(recvm.dtype)
+        for c in range(CHUNKS):
+            recvm[c][g, slots] = jnp.full((deep, tile), -32768, jnp.int32).astype(sendm.dtype)
+    for c in range(CHUNKS):
+        ownm[c, slots] = jnp.zeros((deep, tile), jnp.float32)
     all_cols = cols[0]
     lane = lax.broadcasted_iota(jnp.int32, (groups, LANES), 1)
     row = lax.broadcasted_iota(jnp.int32, (groups, LANES), 0)
@@ -188,18 +193,23 @@
 
     loop(0, me, small_sends)
 
-    def mirror_send(h):
+    def mirror_send(h, c):
         return remote(
-            sendm.at[h], recvm.at[me, pl.ds(0, slots)], m_s.at[h], m_r.at[me], group_peer(h)
+            sendm.at[h, c], recvm[c].at[me, pl.ds(0, slots)], m_s.at[h, c], m_r.at[me, c], group_peer(h)
         )
 
     def mirror(h):
         block_copy(h).wait()
         for s in range(slots):
             product = jnp.dot(factor[...], tiles[h, s], preferred_element_type=jnp.float32)
-            coded = jnp.round(product * to_levels - OFFSET)
-            sendm[h, s] = coded.astype(jnp.int32).astype(sendm.dtype)
-        mirror_send(h).start()
+            coded = jnp.round(product * to_levels - OFFSET).astype(jnp.int32).astype(sendm.dtype)
+            for c in range(CHUNKS):
+                sendm[h, c, s] = coded[c * deep : (c + 1) * deep]
+        mirror_send(h, 0).start()
+
+    loop(0, me, mirror)
+    for chunk in range(1, CHUNKS):
+        loop(0, me, lambda h: mirror_send(h, chunk).start())
 
     def forward(i):
         z = z_other(i)
@@ -208,16 +218,7 @@
         y_send(z, hall.at[p]).start()
         c_send(ry, z, hall.at[p]).start()
 
-    def first_step(i):
-        @pl.when(i < me)
-        def _():
-            mirror(i)
-
-        @pl.when(i < nrz - 1)
-        def _():
-            forward(i)
-
-    loop(0, max(groups - 1, nrz - 1), first_step)
+    loop(0, nrz - 1, forward)
 
     def second_step(i):
         z = (rz + i) % nrz
@@ -260,7 +261,9 @@
     block_copy(me).wait()
     lower[...] = jnp.zeros((rank, tile), jnp.float32)
     for s in range(slots):
-        ownm[s] = jnp.dot(factor[...], tiles[me, s], preferred_element_type=jnp.float32)
+        product = jnp.dot(factor[...], tiles[me, s], preferred_element_type=jnp.float32)
+        for c in range(CHUNKS):
+            ownm[c, s] = product[c * deep : (c + 1) * deep]
         lower[...] += nt_dot(hall[tabs[me, 0, s]], tiles[me, s])
 
     def gram_send(h):
@@ -271,60 +274,80 @@
 
     base[...] = jnp.zeros((rank, tile), jnp.float32)
 
-    def mirror_in(g):
-        remote(sendm.at[0], recvm.at[g, pl.ds(0, slots)], m_s.at[0], m_r.at[g], c_peer).wait_recv()
+    def add_offset(g):
         base[...] += OFFSET * scale[g]
 
-    loop(me + 1, groups, mirror_in)
-
-    def summed(p):
-        def add(g, total):
-            coded = recvm[g, tabs[g, 0, INV_LANE + p]].astype(jnp.int32).astype(jnp.float32)
-            return total + coded * scale[g]
-
-        return lax.fori_loop(me + 1, groups, add, base[...] + ownm[tabs[me, 0, INV_LANE + p]])
-
-    def core_send(j):
-        return remote(cbuf.at[j], crecv.at[j], c_s.at[j], c_r.at[j], c_peer)
-
-    def for_other(j):
-        cbuf[j] = summed(j * nrc + 1 - rc)
-        core_send(j).start()
-
-    def for_this(j):
-        part[j] = summed(j * nrc + rc)
-
-    loop(0, nry * nrz, for_other)
-    loop(0, nry * nrz, for_this)
-
-    def row_y_send(z):
-        return remote(part.at[(1 - ry) * nrz + z], yrecv.at[z], y_s.at[z], y_r.at[z], y_peer)
-
-    def to_y(i):
-        z = (rz + i) % nrz
-        j = (1 - ry) * nrz + z
-        core_send(j).wait_recv()
-        part[j] += crecv[j]
-        row_y_send(z).start()
-
-    loop(0, nrz, to_y)
-
-    def row_z_send(z):
-        return remote(part.at[ry * nrz + z], zrecv.at[rz], z_s.at[z], z_r.at[rz], z_peer(z))
-
-    def to_z(z):
-        j = ry * nrz + z
-        core_send(j).wait_recv()
-        row_y_send(z).wait_recv()
-        part[j] += crecv[j] + yrecv[z]
-
-    def to_z_sent(i):
-        z = z_other(i)
-        to_z(z)
-        row_z_send(z).start()
-
-    loop(0, nrz - 1, to_z_sent)
-    to_z(rz)
+    loop(me + 1, groups, add_offset)
+    other, own = (1 - ry) * nrz, ry * nrz
+
+    def core_send(c, y):
+        first = pl.ds(y * nrz, half)
+        return remote(cbuf.at[c, first], crecv.at[c, first], c_s.at[c, y], c_r.at[c, y], c_peer)
+
+    def row_y_send(c):
+        return remote(part.at[c, pl.ds(other, half)], yrecv.at[c], y_s.at[c], y_r.at[c], y_peer)
+
+    def row_z_send(c, z):
+        return remote(part.at[c, own + z], zrecv.at[c, rz], z_s.at[c, z], z_r.at[c, rz], z_peer(z))
+
+    def sum_chunk(c):
+        rows = slice(c * deep, (c + 1) * deep)
+
+        def mirror_in(g):
+            remote(
+                sendm.at[0, c], recvm[c].at[g, pl.ds(0, slots)], m_s.at[0, c], m_r.at[g, c], c_peer
+            ).wait_recv()
+
+        loop(me + 1, groups, mirror_in)
+
+        def summed(p):
+            def add(g, total):
+                coded = recvm[c][g, tabs[g, 0, INV_LANE + p]].astype(jnp.int32).astype(jnp.float32)
+                return total + coded * scale[g, rows, :]
+
+            start = base[rows, :] + ownm[c, tabs[me, 0, INV_LANE + p]]
+            return lax.fori_loop(me + 1, groups, add, start)
+
+        def for_other_core(j):
+            cbuf[c, j] = summed(j * nrc + 1 - rc)
+
+        def for_this_core(j):
+            part[c, j] = summed(j * nrc + rc)
+
+        loop(other, other + half, for_other_core)
+        core_send(c, 1 - ry).start()
+        loop(own, own + half, for_other_core)
+        core_send(c, ry).start()
+        loop(0, nry * nrz, for_this_core)
+
+    def chunk_to_y(c):
+        core_send(c, 1 - ry).wait_recv()
+
+        def add(j):
+            part[c, j] += crecv[c, j]
+
+        loop(other, other + half, add)
+        row_y_send(c).start()
+
+    def chunk_to_z(c):
+        core_send(c, ry).wait_recv()
+        row_y_send(c).wait_recv()
+
+        def add(z):
+            part[c, own + z] += crecv[c, own + z] + yrecv[c, z]
+
+        def send(i):
+            row_z_send(c, z_other(i)).start()
+
+        loop(0, nrz, add)
+        loop(0, nrz - 1, send)
+
+    for chunk in range(CHUNKS):
+        sum_chunk(chunk)
+        if chunk > 0:
+            chunk_to_z(chunk - 1)
+        chunk_to_y(chunk)
+    chunk_to_z(CHUNKS - 1)
 
     def lower_in(h):
         remote(sendl.at[0], recvl.at[h], l_s.at[0], l_r.at[h], c_peer).wait_recv()
@@ -335,14 +358,18 @@
 
     loop(0, me, lower_in)
 
-    lower[...] += part[ry * nrz + rz]
-
-    def from_z(i):
-        z = z_other(i)
-        remote(part.at[0], zrecv.at[z], z_s.at[0], z_r.at[z], c_peer).wait_recv()
-        lower[...] += zrecv[z]
-
-    loop(0, nrz - 1, from_z)
+    for chunk in range(CHUNKS):
+        rows = slice(chunk * deep, (chunk + 1) * deep)
+        lower[rows, :] += part[chunk, own + rz]
+
+        def from_z(i):
+            z = z_other(i)
+            remote(
+                part.at[chunk, 0], zrecv.at[chunk, z], z_s.at[chunk, 0], z_r.at[chunk, z], c_peer
+            ).wait_recv()
+            lower[rows, :] += zrecv[chunk, z]
+
+        loop(0, nrz - 1, from_z)
     prod_out[...] = lower[...]
 
     def gram_in(g):
@@ -358,7 +385,8 @@
     def sent_down(h):
         table_send(h).wait_send()
         sums_send(h).wait_send()
-        mirror_send(h).wait_send()
+        for c in range(CHUNKS):
+            mirror_send(h, c).wait_send()
         gram_send(h).wait_send()
 
     def sent_up(g):
@@ -371,21 +399,23 @@
     def sent_z(i):
         z = z_other(i)
         z_send(z).wait_send()
-        row_z_send(z).wait_send()
+        for c in range(CHUNKS):
+            row_z_send(c, z).wait_send()
 
     loop(0, nrz - 1, sent_z)
 
     def sent_y(z):
         y_send(z, factor).wait_send()
-        row_y_send(z).wait_send()
 
     loop(0, nrz, sent_y)
 
     def sent_c(j):
         c_send(j // nrz, j % nrz, factor).wait_send()
-        core_send(j).wait_send()
-
     loop(0, nry * nrz, sent_c)
+    for c in range(CHUNKS):
+        row_y_send(c).wait_send()
+        for y in range(nry):
+            core_send(c, y).wait_send()
 
 
 def exchange(sizes, blocks, columns, factor):
@@ -397,6 +427,7 @@
     f32, bf16, i32, i16 = jnp.float32, jnp.bfloat16, jnp.int32, jnp.int16
     dma = pltpu.SemaphoreType.DMA
     one = (rank, tile)
+    deep = (rank // CHUNKS, tile)
     vmem = pl.BlockSpec(memory_space=pltpu.VMEM)
     return pl.pallas_call(
         functools.partial(exchange_kernel, sizes),
@@ -413,26 +444,29 @@
             pltpu.VMEM((groups, 8, LANES), f32),
             pltpu.VMEM((groups, *one), f32),
             pltpu.VMEM(one, f32),
-            pltpu.VMEM((groups, slots, *one), i16),
-            pltpu.VMEM((groups, slots + 1, *one), i16),
-            pltpu.VMEM((slots + 1, *one), f32),
+            pltpu.VMEM((groups, CHUNKS, slots, *deep), i16),
+            [pltpu.VMEM((groups, slots + 1, *deep), i16)] * CHUNKS,
+            pltpu.VMEM((CHUNKS, slots + 1, *deep), f32),
             pltpu.VMEM((groups, slots, *one), bf16),
             pltpu.VMEM((groups, slots, *one), bf16),
             pltpu.VMEM(one, f32),
             pltpu.VMEM((rank, LANES), f32),
             pltpu.VMEM((groups, rank, LANES), f32),
-            pltpu.VMEM((pairs, *one), f32),
-            pltpu.VMEM((pairs, *one), f32),
-            pltpu.VMEM((pairs, *one), f32),
-            pltpu.VMEM((nrz, *one), f32),
-            pltpu.VMEM((nrz, *one), f32),
+            pltpu.VMEM((CHUNKS, pairs, *deep), f32),
+            pltpu.VMEM((CHUNKS, pairs, *deep), f32),
+            pltpu.VMEM((CHUNKS, pairs, *deep), f32),
+            pltpu.VMEM((CHUNKS, nrz, *deep), f32),
+            pltpu.VMEM((CHUNKS, nrz, *deep), f32),
             dma((groups,)),
             dma,
             dma((2 * nrz + pairs,)),
             dma((rows_grp,)),
-            *[dma((groups,))] * 10,
-            *[dma((pairs,))] * 2,
-            *[dma((nrz,))] * 4,
+            *[dma((groups,))] * 4,
+            *[dma((groups, CHUNKS))] * 2,
+            *[dma((groups,))] * 4,
+            *[dma((CHUNKS, nry))] * 2,
+            *[dma((CHUNKS,))] * 2,
+            *[dma((CHUNKS, nrz))] * 2,
         ],
         compiler_params=pltpu.CompilerParams(
             collective_id=0, has_side_effects=True, vmem_limit_bytes=48 * 1024 * 1024

time: 84.1 us -> 67.1 us (0.80)
  the two profiles are of different devices: /device:TPU:60 before, /device:TPU:32 now
where the time goes in v2:
time: 67.1 us; the launch traced here: 66.9 us
  Pallas kernels  64.2 us (96%)
  local copies, waits for them, and re-layouts  2.66 us (4%)
    pallas_call x1, Pallas kernels, exchange(): pl.pallas_call(functools.partial(exchange_kernel, sizes), out_shape=(jax....  62 us
    unnamed x8, local copies, waits for them, and re-layouts  2.66 us
    pallas_call x1, Pallas kernels, sweep(): pl.pallas_call(sweep_kernel, out_shape=jax.ShapeDtypeStruct(factor.shape,...  2.23 us

profile of v2, /device:TPU:32, one launch (start us, length us, event | category | flops | bytes accessed | tf_op | source)
XLA Modules:
  0.0 66.9 jit_solution(2114549770898359077)
XLA Ops:
  0.0 0.0 copy-start
  0.0 0.8 %copy-done = bf16[64,256]{1,0:T(8,128)(2,1)S(1)} copy-done((bf16[64,256]{1,0:T(8,128)(2,1)S(1)}, bf16[64,256]{1,0:T(8,128)(2,1)}, u32[]{:S(2)}) %copy-start) | copy-done | bytes 32792
  0.8 0.0 copy-start.3
  0.8 0.7 %copy-done.3 = s32[1,8,10]{2,1,0:T(8,128)S(1)} copy-done((s32[1,8,10]{2,1,0:T(8,128)S(1)}, s32[1,8,10]{2,1,0:T(8,128)}, u32[]{:S(2)}) %copy-start.3) | copy-done | bytes 344
  1.4 62.0 %exchange.1 = (f32[64,256]{1,0:T(8,128)S(1)}, f32[64,128]{1,0:T(8,128)S(1)}) custom-call(bf16[1,8,10,256,256]{4,3,2,1,0:T(8,128)(2,1)} %blocks.1, s32[1,8,10]{2,1,0:T(8,128)S(1)} %copy-done.3, bf16[64,256]{1,0:T(8,128)(2,1)S(1)} %copy-done), custom_call_target="tpu_custom_call" | custom-call | tf_op jit(solution)/shard_map/exchange/pallas_call | solution.py:432
  63.4 0.0 copy-start.1
  63.4 0.6 copy-done.1
  64.0 0.0 copy-start.2
  64.0 0.6 copy-done.2
  64.6 2.2 %sweep.1 = f32[64,256]{1,0:T(8,128)} custom-call(f32[64,256]{1,0:T(8,128)} %copy-done.1, f32[64,128]{1,0:T(8,128)} %copy-done.2, bf16[64,256]{1,0:T(8,128)(2,1)} %factor.3), custom_call_target="tpu_custom_call" | custom-call | tf_op jit(solution)/shard_map/sweep/pallas_call | solution.py:507
Async XLA Ops:
  0.0 0.8 %copy-start = (bf16[64,256]{1,0:T(8,128)(2,1)S(1)}, bf16[64,256]{1,0:T(8,128)(2,1)}, u32[]{:S(2)}) copy-start(bf16[64,256]{1,0:T(8,128)(2,1)} %factor.3) | copy-start | bytes 98308
  0.8 0.7 %copy-start.3 = (s32[1,8,10]{2,1,0:T(8,128)S(1)}, s32[1,8,10]{2,1,0:T(8,128)}, u32[]{:S(2)}) copy-start(s32[1,8,10]{2,1,0:T(8,128)} %cols.1) | copy-start | bytes 964
  63.4 0.6 copy-start.1
  64.0 0.6 copy-start.2

commit v3 on v2

v3 whole, which is shorter than its diff:
```python
import functools

import jax
import jax.numpy as jnp
from jax import lax
from jax.experimental import pallas as pl
from jax.experimental.pallas import tpu as pltpu
from jax.sharding import Mesh
from jax.sharding import PartitionSpec as P

AXES = ("grp_0", "grp_1", "row_0", "row_1", "row_2")
BY_MESH = pl.DeviceIdType.MESH
LANES = 128
INV_LANE = 32
CHUNKS = 4
LEVELS = 65534.0
OFFSET = 32768.0
floor_value = 1e-6


def nt_dot(a, b):
    return lax.dot_general(a, b, (((1,), (1,)), ((), ())), preferred_element_type=jnp.float32)


def to_column(row, rank):
    spread = jnp.broadcast_to(row, (rank, LANES))
    lane = lax.broadcasted_iota(jnp.int32, (rank, LANES), 1)
    place = lax.broadcasted_iota(jnp.int32, (rank, LANES), 0)
    return jnp.sum(jnp.where(lane == place, spread, 0.0), axis=1, keepdims=True)


def exchange_kernel(
    sizes,
    blocks,
    cols_in,
    factor_in,
    out,
    cols,
    factor,
    tiles,
    hall,
    hfar,
    tab,
    tabin,
    tabs,
    sums,
    sumsin,
    scale,
    base,
    sendm,
    recvm,
    ownm,
    sendl,
    recvl,
    lower,
    gsend,
    grecv,
    part,
    cbuf,
    crecv,
    yrecv,
    zrecv,
    in_sem,
    blk_sem,
    tab_sem,
    ag_s,
    ag_r,
    far_s,
    far_r,
    seed_s,
    tab_s,
    tab_r,
    sum_s,
    sum_r,
    m_s,
    m_r,
    l_s,
    l_r,
    g_s,
    g_r,
    c_s,
    c_r,
    y_s,
    y_r,
    z_s,
    z_r,
):
    ngx, ngy, nry, nrz, nrc = sizes
    gx, gy, ry, rz, rc = [lax.axis_index(axis) for axis in AXES]
    groups, slots = tiles.shape[0], tiles.shape[1]
    rank, tile = factor.shape
    rows_grp = nry * nrz * nrc
    me = gx * ngy + gy
    far = ngx // 2

    def place(y, z, c):
        return (y * nrz + z) * nrc + c

    mine = place(ry, rz, rc)
    deep = rank // CHUNKS
    half = nrz

    def group_peer(h):
        hx, hy = h // ngy, h % ngy
        flip = (hy - gy) * (hy - gy)
        return (hx, hy, ry + flip - 2 * ry * flip, rz, rc)

    def z_peer(z):
        return (gx, gy, ry, z, rc)

    y_peer = (gx, gy, 1 - ry, rz, rc)
    c_peer = (gx, gy, ry, rz, 1 - rc)

    def z_other(i):
        step = (i // 2 + 1) * (1 - 2 * (i % 2))
        return (rz + step + nrz) % nrz

    def remote(src, dst, send, recv, peer):
        return pltpu.make_async_remote_copy(
            src_ref=src, dst_ref=dst, send_sem=send, recv_sem=recv, device_id=peer, device_id_type=BY_MESH
        )

    def block_copy(h):
        return pltpu.make_async_copy(blocks.at[0, h], tiles.at[h], blk_sem.at[h])

    def loop(start, stop, body):
        def step(i, carry):
            body(i)
            return carry

        lax.fori_loop(start, stop, step, 0)

    cols_copy = pltpu.make_async_copy(cols_in, cols, in_sem.at[0])
    factor_copy = pltpu.make_async_copy(factor_in, factor, in_sem.at[1])
    cols_copy.start()
    factor_copy.start()
    barrier = pltpu.get_barrier_semaphore()

    def greet(peer):
        pl.semaphore_signal(barrier, inc=1, device_id=peer, device_id_type=BY_MESH)

    loop(0, me, lambda h: greet(group_peer(h)))
    loop(me + 1, groups, lambda h: greet(group_peer(h)))
    loop(0, nrz - 1, lambda i: greet(z_peer(z_other(i))))
    greet(y_peer)
    greet(c_peer)
    loop(0, me + 1, lambda h: block_copy(h).start())

    hall[rows_grp] = jnp.zeros((rank, tile), hall.dtype)
    for q in range(ngy):
        hfar[q, rows_grp] = jnp.zeros((rank, tile), hall.dtype)
    for g in range(groups):
        for c in range(CHUNKS):
            recvm[c][g, slots] = jnp.full((deep, tile), -32768, jnp.int32).astype(sendm.dtype)
    for c in range(CHUNKS):
        ownm[c, slots] = jnp.zeros((deep, tile), jnp.float32)
    cols_copy.wait()
    factor_copy.wait()
    hall[mine] = factor[...]
    all_cols = cols[0]
    lane = lax.broadcasted_iota(jnp.int32, (groups, LANES), 1)
    row = lax.broadcasted_iota(jnp.int32, (groups, LANES), 0)
    table = jnp.where(lane >= INV_LANE, slots, rows_grp)
    for s in range(slots):
        column = jnp.broadcast_to(all_cols[:, s : s + 1], (groups, LANES))
        offset = column - row * rows_grp
        live = (offset >= 0) & (offset < rows_grp)
        table = jnp.where(live & (lane == s), offset, table)
        table = jnp.where(live & (lane - INV_LANE == offset), s, table)
    for h in range(groups):
        tab[h] = jnp.broadcast_to(table[h : h + 1], (8, LANES))

    def keep_own(h):
        tabin[h] = tab[h]

    loop(0, me + 1, keep_own)
    row_sums = nt_dot(jnp.ones((8, tile), jnp.bfloat16), factor[...])
    sums[...] = jnp.zeros((8, LANES), jnp.float32)
    sums[:, 0:rank] = jnp.maximum(row_sums, 1e-30)
    to_levels = LEVELS / to_column(sums[0:1, :], rank)

    def mirror_send(h, c):
        return remote(
            sendm.at[h, c], recvm[c].at[me, pl.ds(0, slots)], m_s.at[h, c], m_r.at[me, c], group_peer(h)
        )

    def mirror(h):
        block_copy(h).wait()
        for s in range(slots):
            product = jnp.dot(factor[...], tiles[h, s], preferred_element_type=jnp.float32)
            coded = jnp.round(product * to_levels - OFFSET).astype(jnp.int32).astype(sendm.dtype)
            for c in range(CHUNKS):
                sendm[h, c, s] = coded[c * deep : (c + 1) * deep]

    pl.semaphore_wait(barrier, groups - 1 + nrz - 1 + 2)

    class Gather:
        def __init__(self, held, send, recv, y):
            self.held, self.send, self.recv, self.y = held, send, recv, y
            self.seed = place(y, rz, rc)

        def z_copy(self, z, src):
            p = self.seed
            return remote(src, self.held.at[p], self.send.at[z], self.recv.at[p], z_peer(z))

        def y_copy(self, z, src):
            p = place(self.y, z, rc)
            return remote(src, self.held.at[p], self.send.at[nrz + z], self.recv.at[p], y_peer)

        def c_copy(self, y, z, src):
            p = place(y, z, rc)
            return remote(src, self.held.at[p], self.send.at[(2 + y) * nrz + z], self.recv.at[p], c_peer)

        def arrived(self, p):
            remote(factor, self.held.at[p], self.send.at[0], self.recv.at[p], c_peer).wait_recv()

        def begin(self, src):
            loop(0, nrz - 1, lambda i: self.z_copy(z_other(i), src).start())
            self.y_copy(rz, src).start()
            self.c_copy(self.y, rz, src).start()

        def forward(self, i):
            z = z_other(i)
            p = place(self.y, z, rc)
            self.arrived(p)
            self.y_copy(z, self.held.at[p]).start()
            self.c_copy(self.y, z, self.held.at[p]).start()

        def second(self, i):
            z = (rz + i) % nrz
            p = place(1 - self.y, z, rc)
            self.arrived(p)
            self.c_copy(1 - self.y, z, self.held.at[p]).start()

        def finish(self):
            loop(0, nry * nrz, lambda j: self.arrived(j * nrc + 1 - rc))

        def drain(self):
            loop(0, nrz - 1, lambda i: self.z_copy(z_other(i), factor).wait_send())
            loop(0, nrz, lambda z: self.y_copy(z, factor).wait_send())
            loop(0, nry * nrz, lambda j: self.c_copy(j // nrz, j % nrz, factor).wait_send())

    def flipped(y, q):
        flip = (q - gy) * (q - gy)
        return y + flip - 2 * y * flip

    near_set = Gather(hall, ag_s, ag_r, ry)
    far_sets = [Gather(hfar.at[q], far_s.at[q], far_r.at[q], flipped(ry, q)) for q in range(ngy)]

    def seed_send(q):
        peer = (gx + far, q, flipped(ry, q), rz, rc)
        return remote(factor, hfar.at[gy, mine], seed_s.at[q], far_r.at[gy, mine], peer)

    def when_far(body):
        pl.when(gx >= far)(body)

    near_set.begin(factor)

    @pl.when(gx < far)
    def _():
        for q in range(ngy):
            seed_send(q).start()

    def table_send(h):
        return remote(tab.at[h], tabin.at[me], tab_s.at[h], tab_r.at[me], group_peer(h))

    def sums_send(h):
        return remote(sums, sumsin.at[me], sum_s.at[h], sum_r.at[me], group_peer(h))

    def small_sends(h):
        table_send(h).start()
        sums_send(h).start()

    loop(0, me, small_sends)

    def mirror_late(h):
        mirror(h)
        mirror_send(h, 0).start()

    loop(0, me, mirror_late)
    for chunk in range(1, CHUNKS):
        loop(0, me, lambda h: mirror_send(h, chunk).start())

    block_copy(me).wait()
    for s in range(slots):
        product = jnp.dot(factor[...], tiles[me, s], preferred_element_type=jnp.float32)
        for c in range(CHUNKS):
            ownm[c, s] = product[c * deep : (c + 1) * deep]

    loop(0, nrz - 1, near_set.forward)

    @when_far
    def _():
        for held in far_sets:
            held.arrived(held.seed)
            held.begin(held.held.at[held.seed])

    loop(0, nrz, near_set.second)

    def tables_in(g):
        remote(tab.at[0], tabin.at[g], tab_s.at[0], tab_r.at[g], c_peer).wait_recv()
        remote(sums, sumsin.at[g], sum_s.at[0], sum_r.at[g], c_peer).wait_recv()
        column = to_column(sumsin[g][0:1, :], rank) * (1.0 / LEVELS)
        scale[g] = jnp.broadcast_to(column, (rank, tile))

    loop(me + 1, groups, tables_in)
    to_scalars = pltpu.make_async_copy(tabin, tabs, tab_sem)
    to_scalars.start()
    to_scalars.wait()
    near_set.finish()

    def lower_send(g):
        return remote(sendl.at[g], recvl.at[me], l_s.at[g], l_r.at[me], group_peer(g))

    def serve(g):
        @pl.when(g // ngy != gx + far)
        def _():
            for s in range(slots):
                sendl[g, s] = hall[tabs[g, 0, s]]
            lower_send(g).start()

    loop(me + 1, groups, serve)

    gsend[...] = jnp.zeros((rank, LANES), jnp.float32)

    def gram_part(part_of):
        def step(i, total):
            for p in range(4):
                held = hall[part_of * (rows_grp // 2) + i * 4 + p]
                total += nt_dot(held, held)
            return total

        gsend[:, 0:rank] = lax.fori_loop(0, rows_grp // 8, step, gsend[:, 0:rank])

    def gram_send(h):
        return remote(gsend, grecv.at[me], g_s.at[h], g_r.at[me], group_peer(h))

    def gram_sends():
        grecv[me] = gsend[...]
        loop(0, me, lambda h: gram_send(h).start())
        loop(me + 1, groups, lambda h: gram_send(h).start())

    base[...] = jnp.zeros((rank, tile), jnp.float32)

    def no_scale(g):
        scale[g] = jnp.zeros((rank, tile), jnp.float32)

    loop(0, me + 1, no_scale)
    for g in range(1, groups):
        base[...] += OFFSET * scale[g]
    other, own = (1 - ry) * nrz, ry * nrz

    def core_send(c, y):
        first = pl.ds(y * nrz, half)
        return remote(cbuf.at[c, first], crecv.at[c, first], c_s.at[c, y], c_r.at[c, y], c_peer)

    def row_y_send(c):
        return remote(part.at[c, pl.ds(other, half)], yrecv.at[c], y_s.at[c], y_r.at[c], y_peer)

    def row_z_send(c, z):
        return remote(part.at[c, own + z], zrecv.at[c, rz], z_s.at[c, z], z_r.at[c, rz], z_peer(z))

    def sum_chunk(c):
        rows = slice(c * deep, (c + 1) * deep)

        def mirror_in(g):
            remote(
                sendm.at[0, c], recvm[c].at[g, pl.ds(0, slots)], m_s.at[0, c], m_r.at[g, c], c_peer
            ).wait_recv()

        loop(me + 1, groups, mirror_in)

        def summed(p):
            total = base[rows, :] + ownm[c, tabs[me, 0, INV_LANE + p]]
            for g in range(1, groups):
                slot = jnp.where(g > me, tabs[g, 0, INV_LANE + p], slots)
                total += recvm[c][g, slot].astype(jnp.int32).astype(jnp.float32) * scale[g, rows, :]
            return total

        def for_other_core(j):
            cbuf[c, j] = summed(j * nrc + 1 - rc)

        def for_this_core(j):
            part[c, j] = summed(j * nrc + rc)

        loop(other, other + half, for_other_core)
        core_send(c, 1 - ry).start()
        loop(own, own + half, for_other_core)
        core_send(c, ry).start()
        loop(0, nry * nrz, for_this_core)

    def chunk_to_y(c):
        core_send(c, 1 - ry).wait_recv()

        def add(j):
            part[c, j] += crecv[c, j]

        loop(other, other + half, add)
        row_y_send(c).start()

    def chunk_to_z(c):
        core_send(c, ry).wait_recv()
        row_y_send(c).wait_recv()

        def add(z):
            part[c, own + z] += crecv[c, own + z] + yrecv[c, z]

        def send(i):
            row_z_send(c, z_other(i)).start()

        loop(0, nrz, add)
        loop(0, nrz - 1, send)

    gram_part(0)
    gram_part(1)
    gram_sends()
    for c in range(CHUNKS):
        sum_chunk(c)
        if 1 <= c <= ngy:
            when_far(lambda: loop(0, nrz - 1, far_sets[c - 1].forward))
        if c > 0:
            chunk_to_z(c - 1)
        chunk_to_y(c)
    when_far(lambda: loop(0, nrz, far_sets[0].second))
    chunk_to_z(CHUNKS - 1)
    when_far(lambda: loop(0, nrz, far_sets[1].second))

    def lower_add(h, tile_of):
        total = lower[...]
        for s in range(slots):
            total += nt_dot(tile_of(s), tiles[h, s])
        lower[...] = total

    lower[...] = jnp.zeros((rank, tile), jnp.float32)
    lower_add(me, lambda s: hall[tabs[me, 0, s]])

    @when_far
    def _():
        for held in far_sets:
            held.finish()
        for q in range(ngy):
            h = (gx - far) * ngy + q
            lower_add(h, lambda s: hfar[q, tabs[h, 0, s]])

    def lower_in(h):
        @pl.when(h // ngy != gx - far)
        def _():
            remote(sendl.at[0], recvl.at[h], l_s.at[0], l_r.at[h], c_peer).wait_recv()
            lower_add(h, lambda s: recvl[h, s])

    loop(0, me, lower_in)

    def gram_in(g):
        remote(gsend, grecv.at[g], g_s.at[0], g_r.at[g], c_peer).wait_recv()

    loop(0, me, gram_in)
    loop(me + 1, groups, gram_in)
    total = grecv[0]
    for g in range(1, groups):
        total += grecv[g]
    gram = total[:, 0:rank]

    current = factor[...].astype(jnp.float32)
    fitted = lax.dot_general(
        gram,
        current,
        (((0,), (0,)), ((), ())),
        precision=lax.Precision.HIGHEST,
        preferred_element_type=jnp.float32,
    )
    excess = lower[...] - fitted
    across = lax.broadcasted_iota(jnp.int32, (rank, rank), 1)
    down = lax.broadcasted_iota(jnp.int32, (rank, rank), 0)
    inverse = 1.0 / jnp.sum(jnp.where(across == down, gram, 0.0), axis=1, keepdims=True)
    for chunk in range(CHUNKS):

        def from_z(i):
            z = z_other(i)
            remote(
                part.at[chunk, 0], zrecv.at[chunk, z], z_s.at[chunk, 0], z_r.at[chunk, z], c_peer
            ).wait_recv()
            part[chunk, own + rz] += zrecv[chunk, z]

        loop(0, nrz - 1, from_z)
        begin = chunk * deep % 8
        end = begin + deep
        pieces = [excess[:begin], excess[begin:end] + part[chunk, own + rz], excess[end:]]
        excess = jnp.concatenate([piece for piece in pieces if piece.shape[0]], axis=0)
        for k in range(chunk * deep, (chunk + 1) * deep):
            at = k % 8
            present = current[k : k + 1]
            fresh = jnp.maximum(present + excess[at : at + 1] * inverse[k : k + 1], floor_value)
            out[k : k + 1, :] = fresh
            if k + 1 < rank:
                keep = 8 if at == 7 else 0
                change = fresh - present
                excess = excess[keep:] - gram[k - at + keep :, k : k + 1] * change

    def sent_down(h):
        table_send(h).wait_send()
        sums_send(h).wait_send()
        for c in range(CHUNKS):
            mirror_send(h, c).wait_send()
        gram_send(h).wait_send()

    def sent_up(g):
        gram_send(g).wait_send()

        @pl.when(g // ngy != gx + far)
        def _():
            lower_send(g).wait_send()

    loop(0, me, sent_down)
    loop(me + 1, groups, sent_up)

    def sent_z(i):
        for c in range(CHUNKS):
            row_z_send(c, z_other(i)).wait_send()

    loop(0, nrz - 1, sent_z)
    near_set.drain()

    @pl.when(gx < far)
    def _():
        for q in range(ngy):
            seed_send(q).wait_send()

    @when_far
    def _():
        for held in far_sets:
            held.drain()

    for c in range(CHUNKS):
        row_y_send(c).wait_send()
        for y in range(nry):
            core_send(c, y).wait_send()


def exchange(sizes, blocks, columns, factor):
    _, groups, slots, tile, _ = blocks.shape
    rank = factor.shape[0]
    _, ngy, nry, nrz, nrc = sizes
    rows_grp = nry * nrz * nrc
    pairs = nry * nrz
    f32, bf16, i32, i16 = jnp.float32, jnp.bfloat16, jnp.int32, jnp.int16
    dma = pltpu.SemaphoreType.DMA
    one = (rank, tile)
    deep = (rank // CHUNKS, tile)
    vmem = pl.BlockSpec(memory_space=pltpu.VMEM)
    return pl.pallas_call(
        functools.partial(exchange_kernel, sizes),
        out_shape=jax.ShapeDtypeStruct(one, f32),
        in_specs=[pl.BlockSpec(memory_space=pl.ANY)] * 3,
        out_specs=vmem,
        scratch_shapes=[
            pltpu.VMEM(columns.shape, i32),
            pltpu.VMEM(one, bf16),
            pltpu.VMEM((groups, slots, tile, tile), bf16),
            pltpu.VMEM((rows_grp + 1, *one), bf16),
            pltpu.VMEM((ngy, rows_grp + 1, *one), bf16),
            pltpu.VMEM((groups, 8, LANES), i32),
            pltpu.VMEM((groups, 8, LANES), i32),
            pltpu.SMEM((groups, 8, LANES), i32),
            pltpu.VMEM((8, LANES), f32),
            pltpu.VMEM((groups, 8, LANES), f32),
            pltpu.VMEM((groups, *one), f32),
            pltpu.VMEM(one, f32),
            pltpu.VMEM((groups, CHUNKS, slots, *deep), i16),
            [pltpu.VMEM((groups, slots + 1, *deep), i16)] * CHUNKS,
            pltpu.VMEM((CHUNKS, slots + 1, *deep), f32),
            pltpu.VMEM((groups, slots, *one), bf16),
            pltpu.VMEM((groups, slots, *one), bf16),
            pltpu.VMEM(one, f32),
            pltpu.VMEM((rank, LANES), f32),
            pltpu.VMEM((groups, rank, LANES), f32),
            pltpu.VMEM((CHUNKS, pairs, *deep), f32),
            pltpu.VMEM((CHUNKS, pairs, *deep), f32),
            pltpu.VMEM((CHUNKS, pairs, *deep), f32),
            pltpu.VMEM((CHUNKS, nrz, *deep), f32),
            pltpu.VMEM((CHUNKS, nrz, *deep), f32),
            dma((2,)),
            dma((groups,)),
            dma,
            dma((2 * nrz + pairs,)),
            dma((rows_grp,)),
            dma((ngy, 2 * nrz + pairs)),
            dma((ngy, rows_grp)),
            dma((ngy,)),
            *[dma((groups,))] * 4,
            *[dma((groups, CHUNKS))] * 2,
            *[dma((groups,))] * 4,
            *[dma((CHUNKS, nry))] * 2,
            *[dma((CHUNKS,))] * 2,
            *[dma((CHUNKS, nrz))] * 2,
        ],
        compiler_params=pltpu.CompilerParams(
            collective_id=0, has_side_effects=True, vmem_limit_bytes=48 * 1024 * 1024
        ),
        name="exchange",
    )(blocks, columns, factor)


def solution(mesh):
    groups, rows_grp = mesh.shape["grp"], mesh.shape["row"]
    sizes = (groups // 2, 2, 2, rows_grp // 4, 2)
    split = Mesh(mesh.devices.reshape(sizes), AXES)

    def per_device(blocks, columns, factor):
        return exchange(sizes, blocks, columns, factor)

    placed = (P(AXES, None, None, None, None), P(AXES, None, None), P(None, AXES))
    return jax.shard_map(
        per_device, mesh=split, in_specs=placed, out_specs=P(None, AXES), check_vma=False
    )
```

time: 67.1 us -> 63.8 us (0.951)
  Pallas kernels: 64.2 us -> 61.5 us
    pallas_call x2 -> x1, Pallas kernels: 64.2 us -> 61.5 us  [exchange(): pl.pallas_call(functools.partial(exchange_kernel, sizes), out_shape=jax.S...]
    unnamed x8 -> x5, local copies, waits for them, and re-layouts: 2.66 us -> 2.08 us
where the time goes in v3:
time: 63.8 us; the launch traced here: 63.6 us
  Pallas kernels  61.5 us (96%)
  local copies, waits for them, and re-layouts  2.08 us (3%)
    pallas_call x1, Pallas kernels, exchange(): pl.pallas_call(functools.partial(exchange_kernel, sizes), out_shape=jax.S...  61.5 us
    unnamed x5, local copies, waits for them, and re-layouts  2.08 us

profile of v3, /device:TPU:32, one launch (start us, length us, event | category | flops | bytes accessed | tf_op | source)
XLA Modules:
  0.0 63.6 jit_solution(17886043315970393241)
XLA Ops:
  0.0 0.0 copy-start
  0.0 0.8 %copy-done = bf16[64,256]{1,0:T(8,128)(2,1)S(1)} copy-done((bf16[64,256]{1,0:T(8,128)(2,1)S(1)}, bf16[64,256]{1,0:T(8,128)(2,1)}, u32[]{:S(2)}) %copy-start) | copy-done | bytes 32792
  0.8 0.0 copy-start.1
  0.8 0.7 %copy-done.1 = s32[1,8,10]{2,1,0:T(8,128)S(1)} copy-done((s32[1,8,10]{2,1,0:T(8,128)S(1)}, s32[1,8,10]{2,1,0:T(8,128)}, u32[]{:S(2)}) %copy-start.1) | copy-done | bytes 344
  1.4 61.5 %exchange.1 = f32[64,256]{1,0:T(8,128)S(1)} custom-call(bf16[1,8,10,256,256]{4,3,2,1,0:T(8,128)(2,1)} %blocks.1, s32[1,8,10]{2,1,0:T(8,128)S(1)} %copy-done.1, bf16[64,256]{1,0:T(8,128)(2,1)S(1)} %copy-done), custom_call_target="tpu_custom_call" | custom-call | tf_op jit(solution)/shard_map/exchange/pallas_call | solution.py:550
  63.0 0.6 copy.5
Async XLA Ops:
  0.0 0.8 %copy-start = (bf16[64,256]{1,0:T(8,128)(2,1)S(1)}, bf16[64,256]{1,0:T(8,128)(2,1)}, u32[]{:S(2)}) copy-start(bf16[64,256]{1,0:T(8,128)(2,1)} %factor_in.1) | copy-start | bytes 98308
  0.8 0.7 %copy-start.1 = (s32[1,8,10]{2,1,0:T(8,128)S(1)}, s32[1,8,10]{2,1,0:T(8,128)}, u32[]{:S(2)}) copy-start(s32[1,8,10]{2,1,0:T(8,128)} %cols_in.1) | copy-start | bytes 964

commit v4 on v3

--- a/solution.py
+++ b/solution.py
@@ -411,28 +411,30 @@
         loop(0, nrz, add)
         loop(0, nrz - 1, send)
 
-    gram_part(0)
-    gram_part(1)
-    gram_sends()
+    def lower_add(h, tile_of):
+        total = lower[...]
+        for s in range(slots):
+            total += nt_dot(tile_of(s), tiles[h, s])
+        lower[...] = total
+
     for c in range(CHUNKS):
         sum_chunk(c)
+        if c == 2:
+            lower[...] = jnp.zeros((rank, tile), jnp.float32)
+            lower_add(me, lambda s: hall[tabs[me, 0, s]])
         if 1 <= c <= ngy:
             when_far(lambda: loop(0, nrz - 1, far_sets[c - 1].forward))
+        if c == 0:
+            gram_part(0)
+        if c == 1:
+            gram_part(1)
+            gram_sends()
         if c > 0:
             chunk_to_z(c - 1)
         chunk_to_y(c)
     when_far(lambda: loop(0, nrz, far_sets[0].second))
     chunk_to_z(CHUNKS - 1)
     when_far(lambda: loop(0, nrz, far_sets[1].second))
-
-    def lower_add(h, tile_of):
-        total = lower[...]
-        for s in range(slots):
-            total += nt_dot(tile_of(s), tiles[h, s])
-        lower[...] = total
-
-    lower[...] = jnp.zeros((rank, tile), jnp.float32)
-    lower_add(me, lambda s: hall[tabs[me, 0, s]])
 
     @when_far
     def _():

time: 63.8 us -> 61.9 us (0.970); the launches traced: 63.6 us -> 61 us
  Pallas kernels: 61.5 us -> 58.9 us
    pallas_call x1, Pallas kernels: 61.5 us -> 58.9 us  [exchange(): pl.pallas_call(functools.partial(exchange_kernel, sizes), out_shape=jax.S...]
where the time goes in v4:
time: 61.9 us; the launch traced here: 61 us
  Pallas kernels  58.9 us (95%)
  local copies, waits for them, and re-layouts  2.08 us (3%)
    pallas_call x1, Pallas kernels, exchange(): pl.pallas_call(functools.partial(exchange_kernel, sizes), out_shape=jax.S...  58.9 us
    unnamed x5, local copies, waits for them, and re-layouts  2.08 us

profile of v4, /device:TPU:32, one launch (start us, length us, event | category | flops | bytes accessed | tf_op | source)
XLA Modules:
  0.0 61.0 jit_solution(5489192229870937903)
XLA Ops:
  0.0 0.0 copy-start
  0.0 0.8 %copy-done = bf16[64,256]{1,0:T(8,128)(2,1)S(1)} copy-done((bf16[64,256]{1,0:T(8,128)(2,1)S(1)}, bf16[64,256]{1,0:T(8,128)(2,1)}, u32[]{:S(2)}) %copy-start) | copy-done | bytes 32792
  0.8 0.0 copy-start.1
  0.8 0.7 %copy-done.1 = s32[1,8,10]{2,1,0:T(8,128)S(1)} copy-done((s32[1,8,10]{2,1,0:T(8,128)S(1)}, s32[1,8,10]{2,1,0:T(8,128)}, u32[]{:S(2)}) %copy-start.1) | copy-done | bytes 344
  1.4 58.9 %exchange.1 = f32[64,256]{1,0:T(8,128)S(1)} custom-call(bf16[1,8,10,256,256]{4,3,2,1,0:T(8,128)(2,1)} %blocks.1, s32[1,8,10]{2,1,0:T(8,128)S(1)} %copy-done.1, bf16[64,256]{1,0:T(8,128)(2,1)S(1)} %copy-done), custom_call_target="tpu_custom_call" | custom-call | tf_op jit(solution)/shard_map/exchange/pallas_call | solution.py:552
  60.4 0.6 %copy.5 = f32[64,256]{1,0:T(8,128)} copy(f32[64,256]{1,0:T(8,128)S(1)} %exchange.1) | data formatting | bytes 131072
Async XLA Ops:
  0.0 0.8 %copy-start = (bf16[64,256]{1,0:T(8,128)(2,1)S(1)}, bf16[64,256]{1,0:T(8,128)(2,1)}, u32[]{:S(2)}) copy-start(bf16[64,256]{1,0:T(8,128)(2,1)} %factor_in.1) | copy-start | bytes 98308
  0.8 0.7 %copy-start.1 = (s32[1,8,10]{2,1,0:T(8,128)S(1)}, s32[1,8,10]{2,1,0:T(8,128)}, u32[]{:S(2)}) copy-start(s32[1,8,10]{2,1,0:T(8,128)} %cols_in.1) | copy-start | bytes 964
